TPU v7x, 32 devices: a whole 2x2x4 slice. The times are simulated.
32 devices in a mesh: gx: 4 (over y, core), gy: 2 (over x), gz: 4 (over z).
Axes of the slice: x: 2, y: 2, z: 4, core: 2. Of those that a mesh axis runs over, the one named last changes fastest.
Arguments:
- concentration: bfloat16 [16, 8, 16, 512], P(None, 'gx', 'gy', 'gz'), may hold values from -8.25 to 11.25
- pressure_head: float32 [8, 16, 512], P('gx', 'gy', 'gz'), may hold values from -4 to -0.5
- zone_ids: int32 [8, 16, 512], P('gx', 'gy', 'gz'), may hold values from 0 to 7
- well_cells: int32 [8, 16, 512], P('gx', 'gy', 'gz'), may hold values 0 or 1
- zone_conductivity: float32 [8], replicated, may hold values from 0.4 to 1
- zone_alpha: float32 [8], replicated, may hold values from 0.05 to 0.35
- disp_molecular: float32 [16], replicated, may hold values from 0.05 to 0.5
- disp_longitudinal: float32 [16], replicated, may hold values from 0.1 to 1
- entry_counts: int32 [4, 2, 4], P('gx', 'gy', 'gz'), may hold values from 40 to 64, as said below
- dest_tiles: int32 [4, 2, 4, 64], P('gx', 'gy', 'gz'), may hold values from 0 to 15
- source_devices: int32 [4, 2, 4, 64, 1], P('gx', 'gy', 'gz'), may hold values from 0 to 7; in each aligned block of 64 rows (0 to 63, 64 to 127, ..., all dimensions but the last counted through in order) at most 8 rows name the same one
- source_tiles: int32 [4, 2, 4, 64], P('gx', 'gy', 'gz'), may hold values from 0 to 15
- interp_weights: bfloat16 [4, 2, 4, 64, 128, 128], P('gx', 'gy', 'gz'), may hold values from -0.0625 to 0.0625
Outputs:
- head_next: float32 [8, 16, 512], P('gx', 'gy', 'gz')
- solute_next: float32 [16, 8, 16, 512], P(None, 'gx', 'gy', 'gz')
Inputs may be any that keep to these rules, and one draw needn't show every extreme that they name: `entry_counts`: some blocks hold all 64 entries live, at least one block in every draw; the others between 40 and 56. `source_devices`: p = gx index * 2 + gy index of the upstream block; among one block's 64 entries no upstream block is named more than 8 times.
All inputs are finite; a program needn't handle non-finite values. No bound on the sum of `well_cells` on one device may be relied on, other than what follows from the above.
Results may differ from a plain program's by a relative error of at most 0.0003.
Values may be sent and summed in bfloat16 or wider, within the bound.
No kernel may reach another device: no remote copies, remote signals or barrier semaphores. Data moves between devices by JAX's collectives and lax.ppermute only.
A program may use at most 64 MiB of HBM per device.

v0:
```python
import jax
import jax.numpy as jnp
from jax import lax
from jax.sharding import PartitionSpec as P

RSTEPS = 2
CG_ITERS = 2


time_step = 0.15
pump_rate = 1.0
disp_time = 1.0
gravity_sign = (0.0, 0.0, 0.0, 0.0, 1.0, -1.0)


def padded_2(x, sides, width):
    for axis, dim in sides:
        count, length = (lax.axis_size(axis), x.shape[dim])
        up = [(i, (i + 1) % count) for i in range(count - 1)]
        down = [(j, i) for i, j in up]
        last = lax.slice_in_dim(x, length - width, length, axis=dim)
        initial = lax.slice_in_dim(x, 0, width, axis=dim)
        before = lax.ppermute(last, axis, up)
        after = lax.ppermute(initial, axis, down)
        x = jnp.concatenate([before, x, after], axis=dim)
    return x


def neighbours(padded):
    return [
        padded[..., 2:, 1:-1, 1:-1],
        padded[..., :-2, 1:-1, 1:-1],
        padded[..., 1:-1, 2:, 1:-1],
        padded[..., 1:-1, :-2, 1:-1],
        padded[..., 1:-1, 1:-1, 2:],
        padded[..., 1:-1, 1:-1, :-2],
    ]


def richards_terms(head_padded, cond_padded):
    head_centre = head_padded[..., 1:-1, 1:-1, 1:-1]
    cond_centre = cond_padded[..., 1:-1, 1:-1, 1:-1]
    net_inflow = jnp.zeros_like(head_centre)
    flux_terms = []
    for face_index, (head_beside, cond_beside) in enumerate(
        zip(neighbours(head_padded), neighbours(cond_padded))
    ):
        face_cond = jnp.sqrt(cond_centre * cond_beside)
        inflow = face_cond * (head_beside - head_centre + gravity_sign[face_index])
        net_inflow = net_inflow + inflow
        flux_terms.append(jnp.sqrt(1.0 + inflow * inflow))
    return (net_inflow, jnp.stack(flux_terms))


def apply_operator(field, flux_terms, mol_coeff, long_coeff):
    padded = padded_2(field, (("gx", 1), ("gy", 2), ("gz", 3)), 1)
    plain_sum = jnp.zeros_like(field)
    weighted = jnp.zeros_like(field)
    for face_index, beside in enumerate(neighbours(padded)):
        difference = field - beside
        plain_sum = plain_sum + difference
        weighted = weighted + flux_terms[face_index] * difference
    return field + disp_time * (mol_coeff * plain_sum + long_coeff * weighted)


def spread(values):
    return values[:, None, None, None]


def squares_total(residual):
    return lax.psum(jnp.sum(residual * residual, axis=(1, 2, 3)), ("gx", "gy", "gz"))


def shards(
    concentration,
    pressure_head,
    zone_ids,
    well_cells,
    zone_conductivity,
    zone_alpha,
    disp_molecular,
    disp_longitudinal,
    entry_counts,
    dest_tiles,
    source_devices,
    source_tiles,
    interp_weights,
):
    zone_range = jnp.arange(zone_conductivity.shape[0], dtype=jnp.int32)
    zone_onehot = (zone_ids[None] == zone_range[:, None, None, None]).astype(jnp.float32)
    cell_cond = jnp.sum(zone_onehot * zone_conductivity[:, None, None, None], axis=0)
    cell_alpha = jnp.sum(zone_onehot * zone_alpha[:, None, None, None], axis=0)
    pumping = well_cells.astype(jnp.float32)
    head_now = pressure_head
    flux_terms = None
    for sweep_index in range(RSTEPS):
        conduct = cell_cond * jnp.exp(cell_alpha * head_now)
        padded = padded_2(jnp.stack([head_now, conduct]), (("gx", 1), ("gy", 2), ("gz", 3)), 1)
        net_inflow, flux_terms = richards_terms(padded[0], padded[1])
        head_now = head_now + time_step * (net_inflow - pump_rate * pumping)
    solutes, cells_x, cells_y, tile_len = concentration.shape
    tile_count = cells_x * cells_y
    entries = dest_tiles.shape[-1]
    peer_count = lax.axis_size("gx") * lax.axis_size("gy")
    slot_count = max(2, (entries + peer_count - 1) // peer_count)
    tile_field = concentration.reshape(solutes, tile_count, tile_len)
    dest_tile = dest_tiles.reshape(entries)
    source_dev = source_devices.reshape(entries)
    source_tile = source_tiles.reshape(entries)
    live_count = entry_counts.reshape(())
    weight_stack = interp_weights.reshape(entries, tile_len, tile_len)
    entry_ids = jnp.arange(entries, dtype=jnp.int32)
    earlier = entry_ids[None, :] < entry_ids[:, None]
    slot_rank = jnp.sum(
        ((source_dev[None, :] == source_dev[:, None]) & earlier).astype(jnp.int32), axis=1
    )
    peer_ids = jnp.arange(peer_count, dtype=jnp.int32)
    slot_ids = jnp.arange(slot_count, dtype=jnp.int32)
    matched = (source_dev[None, None, :] == peer_ids[:, None, None]) & (
        slot_rank[None, None, :] == slot_ids[None, :, None]
    )
    wanted = jnp.sum(jnp.where(matched, source_tile[None, None, :], 0), axis=2)
    asked_ids = lax.all_to_all(wanted, ("gx", "gy"), split_axis=0, concat_axis=0, tiled=True)
    outgoing = jnp.take(tile_field, asked_ids.reshape(peer_count * slot_count), axis=1)
    outgoing = outgoing.reshape(solutes, peer_count, slot_count, tile_len)
    arrived = lax.all_to_all(outgoing, ("gx", "gy"), split_axis=1, concat_axis=1, tiled=True)
    arrived_flat = arrived.reshape(solutes, peer_count * slot_count, tile_len)
    fetched = jnp.take(arrived_flat, source_dev * slot_count + slot_rank, axis=1)
    interpolated = jnp.einsum(
        "set,eto->seo", fetched, weight_stack, preferred_element_type=jnp.float32
    )
    alive_mask = (entry_ids < live_count).astype(jnp.float32)
    tile_ids = jnp.arange(tile_count, dtype=jnp.int32)
    dest_onehot = (dest_tile[None, :] == tile_ids[:, None]).astype(jnp.float32)
    tile_added = jnp.einsum(
        "te,seo->sto",
        dest_onehot,
        interpolated * alive_mask[None, :, None],
        precision=lax.Precision.HIGHEST,
    )
    advected = concentration.astype(jnp.float32) + tile_added.reshape(
        solutes, cells_x, cells_y, tile_len
    )
    mol_coeff = spread(disp_molecular)
    long_coeff = spread(disp_longitudinal)
    solution = jnp.zeros_like(advected)
    residual = advected
    direction = advected
    norm_now = squares_total(residual)
    for iteration in range(CG_ITERS):
        image = apply_operator(direction, flux_terms, mol_coeff, long_coeff)
        curvature = lax.psum(jnp.sum(direction * image, axis=(1, 2, 3)), ("gx", "gy", "gz"))
        step_size = norm_now / curvature
        solution = solution + spread(step_size) * direction
        residual = residual - spread(step_size) * image
        norm_next = squares_total(residual)
        direction = residual + spread(norm_next / norm_now) * direction
        norm_now = norm_next
    return (head_now, solution)


def solution(mesh):
    in_specs = (
        P(None, "gx", "gy", "gz"),
        P("gx", "gy", "gz"),
        P("gx", "gy", "gz"),
        P("gx", "gy", "gz"),
        P(),
        P(),
        P(),
        P(),
        P("gx", "gy", "gz"),
        P("gx", "gy", "gz", None),
        P("gx", "gy", "gz", None, None),
        P("gx", "gy", "gz", None),
        P("gx", "gy", "gz", None, None, None),
    )
    out_specs = (P("gx", "gy", "gz"), P(None, "gx", "gy", "gz"))
    return jax.shard_map(shards, mesh=mesh, in_specs=in_specs, out_specs=out_specs, check_vma=False)
```

profile of v0, /device:TPU:0, one launch (start us, length us, event | category | flops | bytes accessed | tf_op | source)
XLA Modules:
  0.0 260.3 jit_solution(10906592978750760379)
XLA Ops:
  0.6 1.0 convert_reduce_fusion
  1.6 0.7 iota_compare_fusion.3
  2.3 1.5 select_reduce_fusion.2
  3.8 5.2 %all-to-all-start = ((s32[8,1,8]{2,1,0:T(1,128)}), s32[8,1,8]{2,1,0:T(1,128)S(1)}, u32[]{:S(2)}, u32[]{:S(2)}) async-start(s32[8,1,8]{2,1,0:T(1,128)} %bitcast.11), calls=%async_computation | async-start | bytes 8192 | tf_op jit(solution)/shard_map/all_to_all | solution.py:123
  9.0 0.8 select_reduce_fusion
  9.8 0.7 multiply_bitcast_fusion.1
  10.5 0.7 fusion.29
  11.2 2.4 collective-permute-start
  13.6 1.3 collective-permute-start.1
  15.5 0.7 compare_convert_fusion
  16.2 0.7 fusion.70
  16.9 0.9 copy.20
  17.8 0.8 pad_maximum_fusion.57
  18.6 3.5 %collective-permute-start.2 = (f32[2,4,1,128]{3,2,1,0:T(1,128)S(1)}, f32[2,4,1,128]{3,2,1,0:T(1,128)S(1)}, u32[]{:S(2)}, u32[]{:S(2)}) collective-permute-start(f32[2,4,1,128]{3,2,1,0:T(1,128)S(1)} %get-tuple-element.53), channel_id=1, source_target_pairs={{0,4},{1,5},{2,6},{3,7},{8,12},{9,13},{10,14},{11,15},{16,20},{17,... | collective-permute-start | bytes 12296 | tf_op jit(solution)/shard_map/ppermute | solution.py:23
  22.1 1.3 collective-permute-start.3
  23.9 0.7 reduce.3
  24.6 2.9 %collective-permute-done.3 = f32[2,4,1,128]{3,2,1,0:T(1,128)S(1)} collective-permute-done((f32[2,4,1,128]{3,2,1,0:T(1,128)S(1)}, f32[2,4,1,128]{3,2,1,0:T(1,128)S(1)}, u32[]{:S(2)}, u32[]{:S(2)}) %collective-permute-start.3) | collective-permute-done | bytes 4128 | tf_op jit(solution)/shard_map/ppermute | solution.py:24
  27.6 0.7 pad_maximum_fusion.40
  28.4 3.5 %collective-permute-start.4 = (f32[2,4,10,1]{3,2,1,0:T(8,128)S(1)}, f32[2,4,10,1]{3,2,1,0:T(8,128)S(1)}, u32[]{:S(2)}, u32[]{:S(2)}) collective-permute-start(f32[2,4,10,1]{3,2,1,0:T(8,128)S(1)} %get-tuple-element.49), channel_id=1, source_target_pairs={{0,1},{1,2},{2,3},{4,5},{5,6},{6,7},{8,9},{9,10},{10,11},{12,13},{... | collective-permute-start | bytes 968 | tf_op jit(solution)/shard_map/ppermute | solution.py:23
  31.8 1.3 collective-permute-start.5
  33.2 1.0 collective-permute-done.4
  34.2 4.1 %collective-permute-done.5 = f32[2,4,10,1]{3,2,1,0:T(8,128)S(1)} collective-permute-done((f32[2,4,10,1]{3,2,1,0:T(8,128)S(1)}, f32[2,4,10,1]{3,2,1,0:T(8,128)S(1)}, u32[]{:S(2)}, u32[]{:S(2)}) %collective-permute-start.5) | collective-permute-done | bytes 352 | tf_op jit(solution)/shard_map/ppermute | solution.py:24
  38.3 0.8 pad_maximum_fusion.38
  39.2 0.8 multiply_bitcast_fusion
  40.0 1.6 collective-permute-start.6
  41.6 1.3 collective-permute-start.7
  43.0 0.6 gather_fusion
  43.6 4.4 %collective-permute-done.7 = f32[2,1,8,128]{3,2,1,0:T(8,128)S(1)} collective-permute-done((f32[2,1,8,128]{3,2,1,0:T(8,128)S(1)}, f32[2,1,8,128]{3,2,1,0:T(8,128)S(1)}, u32[]{:S(2)}, u32[]{:S(2)}) %collective-permute-start.7) | collective-permute-done | bytes 8224 | tf_op jit(solution)/shard_map/ppermute | solution.py:24
  48.0 1.6 collective-permute-start.8
  49.7 1.3 collective-permute-start.9
  51.0 0.8 broadcast_select_fusion
  51.8 5.7 %all-to-all-start.1 = ((bf16[16,8,8,128]{3,0,2,1:T(8,128)(2,1)}), bf16[16,8,8,128]{3,0,2,1:T(8,128)(2,1)S(1)}, u32[]{:S(2)}, u32[]{:S(2)}) async-start(bf16[16,8,8,128]{3,0,2,1:T(8,128)(2,1)} %broadcast_select_fusion), calls=%async_computation.1 | async-start | bytes 524288 | tf_op jit(solution)/shard_map/all_to_all | solution.py:126
  57.6 3.5 %collective-permute-start.10 = (f32[2,4,10,1]{3,2,1,0:T(8,128)S(1)}, f32[2,4,10,1]{3,2,1,0:T(8,128)S(1)}, u32[]{:S(2)}, u32[]{:S(2)}) collective-permute-start(f32[2,4,10,1]{3,2,1,0:T(8,128)S(1)} %get-tuple-element.47), channel_id=1, source_target_pairs={{0,1},{1,2},{2,3},{4,5},{5,6},{6,7},{8,9},{9,10},{10,11},{12,13},{... | collective-permute-start | bytes 968 | tf_op jit(solution)/shard_map/ppermute | solution.py:23
  61.1 1.3 collective-permute-start.11
  62.4 0.7 collective-permute-done.10
  63.1 4.2 %collective-permute-done.11 = f32[2,4,10,1]{3,2,1,0:T(8,128)S(1)} collective-permute-done((f32[2,4,10,1]{3,2,1,0:T(8,128)S(1)}, f32[2,4,10,1]{3,2,1,0:T(8,128)S(1)}, u32[]{:S(2)}, u32[]{:S(2)}) %collective-permute-start.11) | collective-permute-done | bytes 352 | tf_op jit(solution)/shard_map/ppermute | solution.py:24
  67.5 0.6 gather_fusion.1
  68.1 0.7 fusion.5
  69.3 1.3 collective-permute-start.13
  70.6 1.3 collective-permute-start.12
  71.9 4.1 %collective-permute-done.12 = f32[16,1,8,128]{3,2,1,0:T(8,128)S(1)} collective-permute-done((f32[16,1,8,128]{3,2,1,0:T(8,128)S(1)}, f32[16,1,8,128]{3,2,1,0:T(8,128)S(1)}, u32[]{:S(2)}, u32[]{:S(2)}) %collective-permute-start.12) | collective-permute-done | bytes 65568 | tf_op jit(solution)/shard_map/ppermute | solution.py:24
  76.0 3.4 %collective-permute-start.15 = (f32[16,4,1,128]{3,2,1,0:T(1,128)S(1)}, f32[16,4,1,128]{3,2,1,0:T(1,128)S(1)}, u32[]{:S(2)}, u32[]{:S(2)}) collective-permute-start(f32[16,4,1,128]{3,2,1,0:T(1,128)S(1)} %get-tuple-element.29), channel_id=1, source_target_pairs={{0,4},{1,5},{2,6},{3,7},{8,12},{9,13},{10,14},{11,15},{16,20},{17,... | collective-permute-start | bytes 98312 | tf_op jit(solution)/shard_map/ppermute | solution.py:23
  79.4 1.3 collective-permute-start.14
  81.0 4.2 %collective-permute-done.14 = f32[16,4,1,128]{3,2,1,0:T(1,128)S(1)} collective-permute-done((f32[16,4,1,128]{3,2,1,0:T(1,128)S(1)}, f32[16,4,1,128]{3,2,1,0:T(1,128)S(1)}, u32[]{:S(2)}, u32[]{:S(2)}) %collective-permute-start.14) | collective-permute-done | bytes 32800 | tf_op jit(solution)/shard_map/ppermute | solution.py:24
  85.5 1.3 collective-permute-start.16
  86.8 4.6 %collective-permute-start.17 = (f32[16,4,10,1]{3,2,1,0:T(8,128)S(1)}, f32[16,4,10,1]{3,2,1,0:T(8,128)S(1)}, u32[]{:S(2)}, u32[]{:S(2)}) collective-permute-start(f32[16,4,10,1]{3,2,1,0:T(8,128)S(1)} %get-tuple-element.26), channel_id=1, source_target_pairs={{0,1},{1,2},{2,3},{4,5},{5,6},{6,7},{8,9},{9,10},{10,11},{12,13},{... | collective-permute-start | bytes 7688 | tf_op jit(solution)/shard_map/ppermute | solution.py:23
  91.5 10.2 %collective-permute-done.16 = f32[16,4,10,1]{3,2,1,0:T(8,128)S(1)} collective-permute-done((f32[16,4,10,1]{3,2,1,0:T(8,128)S(1)}, f32[16,4,10,1]{3,2,1,0:T(8,128)S(1)}, u32[]{:S(2)}, u32[]{:S(2)}) %collective-permute-start.16) | collective-permute-done | bytes 2592 | tf_op jit(solution)/shard_map/ppermute | solution.py:24
  101.7 1.7 collective-permute-done.17
  103.4 0.6 multiply_reduce_fusion.1
  104.0 40.4 %all-reduce = (f32[16]{0:T(128)S(1)}, f32[16]{0:T(128)S(1)}) all-reduce(f32[16]{0:T(128)S(1)} %get-tuple-element.3, f32[16]{0:T(128)S(1)} %get-tuple-element.2), channel_id=1, replica_groups=mesh['gx'=4,'gy'=2,'gz'=4] {'gx','gy','gz'}, use_global_device_ids=true, to_apply=%region_5.6 | all-reduce | flops 32 | bytes 256 | tf_op jit(solution)/shard_map/psum | solution.py:71
  144.7 38.1 %psum.30 = f32[16]{0:T(128)S(1)} all-reduce(f32[16]{0:T(128)S(1)} %multiply_reduce_fusion), channel_id=1, replica_groups=mesh['gx'=4,'gy'=2,'gz'=4] {'gx','gy','gz'}, use_global_device_ids=true, to_apply=%region_9.10 | all-reduce | flops 16 | bytes 128 | tf_op jit(solution)/shard_map/psum | solution.py:71
  182.9 1.3 collective-permute-start.19
  184.2 1.3 collective-permute-start.18
  185.5 4.3 %collective-permute-done.18 = f32[16,1,8,128]{3,2,1,0:T(8,128)S(1)} collective-permute-done((f32[16,1,8,128]{3,2,1,0:T(8,128)S(1)}, f32[16,1,8,128]{3,2,1,0:T(8,128)S(1)}, u32[]{:S(2)}, u32[]{:S(2)}) %collective-permute-start.18) | collective-permute-done | bytes 65568 | tf_op jit(solution)/shard_map/ppermute | solution.py:24
  189.9 3.7 %collective-permute-start.21 = (f32[16,4,1,128]{3,2,1,0:T(1,128)S(1)}, f32[16,4,1,128]{3,2,1,0:T(1,128)S(1)}, u32[]{:S(2)}, u32[]{:S(2)}) collective-permute-start(f32[16,4,1,128]{3,2,1,0:T(1,128)S(1)} %get-tuple-element.27), channel_id=1, source_target_pairs={{0,4},{1,5},{2,6},{3,7},{8,12},{9,13},{10,14},{11,15},{16,20},{17,... | collective-permute-start | bytes 98312 | tf_op jit(solution)/shard_map/ppermute | solution.py:23
  193.6 1.3 collective-permute-start.20
  195.2 4.2 %collective-permute-done.20 = f32[16,4,1,128]{3,2,1,0:T(1,128)S(1)} collective-permute-done((f32[16,4,1,128]{3,2,1,0:T(1,128)S(1)}, f32[16,4,1,128]{3,2,1,0:T(1,128)S(1)}, u32[]{:S(2)}, u32[]{:S(2)}) %collective-permute-start.20) | collective-permute-done | bytes 32800 | tf_op jit(solution)/shard_map/ppermute | solution.py:24
  199.7 1.3 collective-permute-start.22
  201.0 4.7 %collective-permute-start.23 = (f32[16,4,10,1]{3,2,1,0:T(8,128)S(1)}, f32[16,4,10,1]{3,2,1,0:T(8,128)S(1)}, u32[]{:S(2)}, u32[]{:S(2)}) collective-permute-start(f32[16,4,10,1]{3,2,1,0:T(8,128)S(1)} %get-tuple-element.24), channel_id=1, source_target_pairs={{0,1},{1,2},{2,3},{4,5},{5,6},{6,7},{8,9},{9,10},{10,11},{12,13},{... | collective-permute-start | bytes 7688 | tf_op jit(solution)/shard_map/ppermute | solution.py:23
  205.7 10.0 %collective-permute-done.22 = f32[16,4,10,1]{3,2,1,0:T(8,128)S(1)} collective-permute-done((f32[16,4,10,1]{3,2,1,0:T(8,128)S(1)}, f32[16,4,10,1]{3,2,1,0:T(8,128)S(1)}, u32[]{:S(2)}, u32[]{:S(2)}) %collective-permute-start.22) | collective-permute-done | bytes 2592 | tf_op jit(solution)/shard_map/ppermute | solution.py:24
  215.7 1.7 collective-permute-done.23
  217.9 0.6 multiply_add_fusion.2
  218.5 41.0 %psum.31 = f32[16]{0:T(128)S(1)} all-reduce(f32[16]{0:T(128)S(1)} %fusion.13), channel_id=1, replica_groups=mesh['gx'=4,'gy'=2,'gz'=4] {'gx','gy','gz'}, use_global_device_ids=true, to_apply=%region_11.12 | all-reduce | flops 16 | bytes 128 | tf_op jit(solution)/shard_map/psum | solution.py:152
  259.5 0.8 multiply_add_fusion
  (55 shorter events, 3.7 us)
Async XLA Ops:
  0.6 67.5 %copy-start = (bf16[1,1,1,64,128,128]{5,4,3,2,1,0:T(8,128)(2,1)S(1)}, bf16[1,1,1,64,128,128]{5,4,3,2,1,0:T(8,128)(2,1)}, u32[]{:S(2)}) copy-start(bf16[1,1,1,64,128,128]{5,4,3,2,1,0:T(8,128)(2,1)} %param.25) | copy-start | bytes 6291460
  3.8 19.6 %all-to-all-start = ((s32[8,1,8]{2,1,0:T(1,128)}), s32[8,1,8]{2,1,0:T(1,128)S(1)}, u32[]{:S(2)}, u32[]{:S(2)}) async-start(s32[8,1,8]{2,1,0:T(1,128)} %bitcast.11), calls=%async_computation | async-start | bytes 8192 | tf_op jit(solution)/shard_map/all_to_all | solution.py:123
  11.2 6.5 %collective-permute-start = (f32[2,1,8,128]{3,2,1,0:T(8,128)S(1)}, f32[2,1,8,128]{3,2,1,0:T(8,128)S(1)}, u32[]{:S(2)}, u32[]{:S(2)}) collective-permute-start(f32[2,1,8,128]{3,2,1,0:T(8,128)S(1)} %get-tuple-element.57), channel_id=1, source_target_pairs={{0,8},{8,16},{16,24},{1,9},{9,17},{17,25},{2,10},{10,18},{18,26},{... | collective-permute-start | bytes 24584 | tf_op jit(solution)/shard_map/ppermute | solution.py:23
  13.6 4.2 %collective-permute-start.1 = (f32[2,1,8,128]{3,2,1,0:T(8,128)S(1)}, f32[2,1,8,128]{3,2,1,0:T(8,128)S(1)}, u32[]{:S(2)}, u32[]{:S(2)}) collective-permute-start(f32[2,1,8,128]{3,2,1,0:T(8,128)S(1)} %get-tuple-element.58), channel_id=1, source_target_pairs={{8,0},{16,8},{24,16},{9,1},{17,9},{25,17},{10,2},{18,10},{26,18},{... | collective-permute-start | bytes 24584 | tf_op jit(solution)/shard_map/ppermute | solution.py:24
  18.6 6.1 %collective-permute-start.2 = (f32[2,4,1,128]{3,2,1,0:T(1,128)S(1)}, f32[2,4,1,128]{3,2,1,0:T(1,128)S(1)}, u32[]{:S(2)}, u32[]{:S(2)}) collective-permute-start(f32[2,4,1,128]{3,2,1,0:T(1,128)S(1)} %get-tuple-element.53), channel_id=1, source_target_pairs={{0,4},{1,5},{2,6},{3,7},{8,12},{9,13},{10,14},{11,15},{16,20},{17,... | collective-permute-start | bytes 12296 | tf_op jit(solution)/shard_map/ppermute | solution.py:23
  22.1 5.5 %collective-permute-start.3 = (f32[2,4,1,128]{3,2,1,0:T(1,128)S(1)}, f32[2,4,1,128]{3,2,1,0:T(1,128)S(1)}, u32[]{:S(2)}, u32[]{:S(2)}) collective-permute-start(f32[2,4,1,128]{3,2,1,0:T(1,128)S(1)} %get-tuple-element.54), channel_id=1, source_target_pairs={{4,0},{5,1},{6,2},{7,3},{12,8},{13,9},{14,10},{15,11},{20,16},{21,... | collective-permute-start | bytes 12296 | tf_op jit(solution)/shard_map/ppermute | solution.py:24
  28.4 5.8 %collective-permute-start.4 = (f32[2,4,10,1]{3,2,1,0:T(8,128)S(1)}, f32[2,4,10,1]{3,2,1,0:T(8,128)S(1)}, u32[]{:S(2)}, u32[]{:S(2)}) collective-permute-start(f32[2,4,10,1]{3,2,1,0:T(8,128)S(1)} %get-tuple-element.49), channel_id=1, source_target_pairs={{0,1},{1,2},{2,3},{4,5},{5,6},{6,7},{8,9},{9,10},{10,11},{12,13},{... | collective-permute-start | bytes 968 | tf_op jit(solution)/shard_map/ppermute | solution.py:23
  31.8 6.5 %collective-permute-start.5 = (f32[2,4,10,1]{3,2,1,0:T(8,128)S(1)}, f32[2,4,10,1]{3,2,1,0:T(8,128)S(1)}, u32[]{:S(2)}, u32[]{:S(2)}) collective-permute-start(f32[2,4,10,1]{3,2,1,0:T(8,128)S(1)} %get-tuple-element.50), channel_id=1, source_target_pairs={{1,0},{2,1},{3,2},{5,4},{6,5},{7,6},{9,8},{10,9},{11,10},{13,12},{... | collective-permute-start | bytes 968 | tf_op jit(solution)/shard_map/ppermute | solution.py:24
  40.0 3.6 %collective-permute-start.6 = (f32[2,1,8,128]{3,2,1,0:T(8,128)S(1)}, f32[2,1,8,128]{3,2,1,0:T(8,128)S(1)}, u32[]{:S(2)}, u32[]{:S(2)}) collective-permute-start(f32[2,1,8,128]{3,2,1,0:T(8,128)S(1)} %get-tuple-element.55), channel_id=1, source_target_pairs={{0,8},{8,16},{16,24},{1,9},{9,17},{17,25},{2,10},{10,18},{18,26},{... | collective-permute-start | bytes 24584 | tf_op jit(solution)/shard_map/ppermute | solution.py:23
  41.6 6.4 %collective-permute-start.7 = (f32[2,1,8,128]{3,2,1,0:T(8,128)S(1)}, f32[2,1,8,128]{3,2,1,0:T(8,128)S(1)}, u32[]{:S(2)}, u32[]{:S(2)}) collective-permute-start(f32[2,1,8,128]{3,2,1,0:T(8,128)S(1)} %get-tuple-element.56), channel_id=1, source_target_pairs={{8,0},{16,8},{24,16},{9,1},{17,9},{25,17},{10,2},{18,10},{26,18},{... | collective-permute-start | bytes 24584 | tf_op jit(solution)/shard_map/ppermute | solution.py:24
  48.0 9.5 %collective-permute-start.8 = (f32[2,4,1,128]{3,2,1,0:T(1,128)S(1)}, f32[2,4,1,128]{3,2,1,0:T(1,128)S(1)}, u32[]{:S(2)}, u32[]{:S(2)}) collective-permute-start(f32[2,4,1,128]{3,2,1,0:T(1,128)S(1)} %get-tuple-element.51), channel_id=1, source_target_pairs={{0,4},{1,5},{2,6},{3,7},{8,12},{9,13},{10,14},{11,15},{16,20},{17,... | collective-permute-start | bytes 12296 | tf_op jit(solution)/shard_map/ppermute | solution.py:23
  49.7 7.8 %collective-permute-start.9 = (f32[2,4,1,128]{3,2,1,0:T(1,128)S(1)}, f32[2,4,1,128]{3,2,1,0:T(1,128)S(1)}, u32[]{:S(2)}, u32[]{:S(2)}) collective-permute-start(f32[2,4,1,128]{3,2,1,0:T(1,128)S(1)} %get-tuple-element.52), channel_id=1, source_target_pairs={{4,0},{5,1},{6,2},{7,3},{12,8},{13,9},{14,10},{15,11},{20,16},{21,... | collective-permute-start | bytes 12296 | tf_op jit(solution)/shard_map/ppermute | solution.py:24
  51.8 15.6 %all-to-all-start.1 = ((bf16[16,8,8,128]{3,0,2,1:T(8,128)(2,1)}), bf16[16,8,8,128]{3,0,2,1:T(8,128)(2,1)S(1)}, u32[]{:S(2)}, u32[]{:S(2)}) async-start(bf16[16,8,8,128]{3,0,2,1:T(8,128)(2,1)} %broadcast_select_fusion), calls=%async_computation.1 | async-start | bytes 524288 | tf_op jit(solution)/shard_map/all_to_all | solution.py:126
  57.5 11.3 %copy-start.1 = (bf16[16,2,8,128]{3,2,1,0:T(8,128)(2,1)S(1)}, bf16[16,2,8,128]{3,2,1,0:T(8,128)(2,1)}, u32[]{:S(2)}) copy-start(bf16[16,2,8,128]{3,2,1,0:T(8,128)(2,1)} %param.13) | copy-start | bytes 196612
  57.5 11.3 %copy-start.5 = (s32[1,1,1,64]{3,2,1,0:T(1,128)S(1)}, s32[1,1,1,64]{3,2,1,0:T(1,128)}, u32[]{:S(2)}) copy-start(s32[1,1,1,64]{3,2,1,0:T(1,128)} %param.22) | copy-start | bytes 772
  57.6 5.5 %collective-permute-start.10 = (f32[2,4,10,1]{3,2,1,0:T(8,128)S(1)}, f32[2,4,10,1]{3,2,1,0:T(8,128)S(1)}, u32[]{:S(2)}, u32[]{:S(2)}) collective-permute-start(f32[2,4,10,1]{3,2,1,0:T(8,128)S(1)} %get-tuple-element.47), channel_id=1, source_target_pairs={{0,1},{1,2},{2,3},{4,5},{5,6},{6,7},{8,9},{9,10},{10,11},{12,13},{... | collective-permute-start | bytes 968 | tf_op jit(solution)/shard_map/ppermute | solution.py:23
  61.1 6.2 %collective-permute-start.11 = (f32[2,4,10,1]{3,2,1,0:T(8,128)S(1)}, f32[2,4,10,1]{3,2,1,0:T(8,128)S(1)}, u32[]{:S(2)}, u32[]{:S(2)}) collective-permute-start(f32[2,4,10,1]{3,2,1,0:T(8,128)S(1)} %get-tuple-element.48), channel_id=1, source_target_pairs={{1,0},{2,1},{3,2},{5,4},{6,5},{7,6},{9,8},{10,9},{11,10},{13,12},{... | collective-permute-start | bytes 968 | tf_op jit(solution)/shard_map/ppermute | solution.py:24
  69.3 34.2 %copy-start.3 = (f32[16]{0:T(128)S(1)}, f32[16]{0:T(128)}, u32[]{:S(2)}) copy-start(f32[16]{0:T(128)} %param.20) | copy-start | bytes 196
  69.3 34.2 %copy-start.4 = (f32[16]{0:T(128)S(1)}, f32[16]{0:T(128)}, u32[]{:S(2)}) copy-start(f32[16]{0:T(128)} %param.19) | copy-start | bytes 196
  69.3 2.6 %collective-permute-start.13 = (f32[16,1,8,128]{3,2,1,0:T(8,128)S(1)}, f32[16,1,8,128]{3,2,1,0:T(8,128)S(1)}, u32[]{:S(2)}, u32[]{:S(2)}) collective-permute-start(f32[16,1,8,128]{3,2,1,0:T(8,128)S(1)} %get-tuple-element.33), channel_id=1, source_target_pairs={{0,8},{8,16},{16,24},{1,9},{9,17},{17,25},{2,10},{10,18},{18,26},{... | collective-permute-start | bytes 196616 | tf_op jit(solution)/shard_map/ppermute | solution.py:23
  70.6 5.4 %collective-permute-start.12 = (f32[16,1,8,128]{3,2,1,0:T(8,128)S(1)}, f32[16,1,8,128]{3,2,1,0:T(8,128)S(1)}, u32[]{:S(2)}, u32[]{:S(2)}) collective-permute-start(f32[16,1,8,128]{3,2,1,0:T(8,128)S(1)} %get-tuple-element.34), channel_id=1, source_target_pairs={{8,0},{16,8},{24,16},{9,1},{17,9},{25,17},{10,2},{18,10},{26,18},{... | collective-permute-start | bytes 196616 | tf_op jit(solution)/shard_map/ppermute | solution.py:24
  76.0 5.0 %collective-permute-start.15 = (f32[16,4,1,128]{3,2,1,0:T(1,128)S(1)}, f32[16,4,1,128]{3,2,1,0:T(1,128)S(1)}, u32[]{:S(2)}, u32[]{:S(2)}) collective-permute-start(f32[16,4,1,128]{3,2,1,0:T(1,128)S(1)} %get-tuple-element.29), channel_id=1, source_target_pairs={{0,4},{1,5},{2,6},{3,7},{8,12},{9,13},{10,14},{11,15},{16,20},{17,... | collective-permute-start | bytes 98312 | tf_op jit(solution)/shard_map/ppermute | solution.py:23
  79.4 5.8 %collective-permute-start.14 = (f32[16,4,1,128]{3,2,1,0:T(1,128)S(1)}, f32[16,4,1,128]{3,2,1,0:T(1,128)S(1)}, u32[]{:S(2)}, u32[]{:S(2)}) collective-permute-start(f32[16,4,1,128]{3,2,1,0:T(1,128)S(1)} %get-tuple-element.30), channel_id=1, source_target_pairs={{4,0},{5,1},{6,2},{7,3},{12,8},{13,9},{14,10},{15,11},{20,16},{21,... | collective-permute-start | bytes 98312 | tf_op jit(solution)/shard_map/ppermute | solution.py:24
  85.5 16.2 %collective-permute-start.16 = (f32[16,4,10,1]{3,2,1,0:T(8,128)S(1)}, f32[16,4,10,1]{3,2,1,0:T(8,128)S(1)}, u32[]{:S(2)}, u32[]{:S(2)}) collective-permute-start(f32[16,4,10,1]{3,2,1,0:T(8,128)S(1)} %get-tuple-element.25), channel_id=1, source_target_pairs={{1,0},{2,1},{3,2},{5,4},{6,5},{7,6},{9,8},{10,9},{11,10},{13,12},{... | collective-permute-start | bytes 7688 | tf_op jit(solution)/shard_map/ppermute | solution.py:24
  86.8 16.6 %collective-permute-start.17 = (f32[16,4,10,1]{3,2,1,0:T(8,128)S(1)}, f32[16,4,10,1]{3,2,1,0:T(8,128)S(1)}, u32[]{:S(2)}, u32[]{:S(2)}) collective-permute-start(f32[16,4,10,1]{3,2,1,0:T(8,128)S(1)} %get-tuple-element.26), channel_id=1, source_target_pairs={{0,1},{1,2},{2,3},{4,5},{5,6},{6,7},{8,9},{9,10},{10,11},{12,13},{... | collective-permute-start | bytes 7688 | tf_op jit(solution)/shard_map/ppermute | solution.py:23
  182.9 2.6 %collective-permute-start.19 = (f32[16,1,8,128]{3,2,1,0:T(8,128)S(1)}, f32[16,1,8,128]{3,2,1,0:T(8,128)S(1)}, u32[]{:S(2)}, u32[]{:S(2)}) collective-permute-start(f32[16,1,8,128]{3,2,1,0:T(8,128)S(1)} %get-tuple-element.31), channel_id=1, source_target_pairs={{0,8},{8,16},{16,24},{1,9},{9,17},{17,25},{2,10},{10,18},{18,26},{... | collective-permute-start | bytes 196616 | tf_op jit(solution)/shard_map/ppermute | solution.py:23
  184.2 5.7 %collective-permute-start.18 = (f32[16,1,8,128]{3,2,1,0:T(8,128)S(1)}, f32[16,1,8,128]{3,2,1,0:T(8,128)S(1)}, u32[]{:S(2)}, u32[]{:S(2)}) collective-permute-start(f32[16,1,8,128]{3,2,1,0:T(8,128)S(1)} %get-tuple-element.32), channel_id=1, source_target_pairs={{8,0},{16,8},{24,16},{9,1},{17,9},{25,17},{10,2},{18,10},{26,18},{... | collective-permute-start | bytes 196616 | tf_op jit(solution)/shard_map/ppermute | solution.py:24
  189.9 5.3 %collective-permute-start.21 = (f32[16,4,1,128]{3,2,1,0:T(1,128)S(1)}, f32[16,4,1,128]{3,2,1,0:T(1,128)S(1)}, u32[]{:S(2)}, u32[]{:S(2)}) collective-permute-start(f32[16,4,1,128]{3,2,1,0:T(1,128)S(1)} %get-tuple-element.27), channel_id=1, source_target_pairs={{0,4},{1,5},{2,6},{3,7},{8,12},{9,13},{10,14},{11,15},{16,20},{17,... | collective-permute-start | bytes 98312 | tf_op jit(solution)/shard_map/ppermute | solution.py:23
  193.6 24.3 %copy-start.2 = (s32[2,8,128]{2,1,0:T(8,128)S(1)}, s32[2,8,128]{2,1,0:T(8,128)}, u32[]{:S(2)}) copy-start(s32[2,8,128]{2,1,0:T(8,128)} %param.16) | copy-start | bytes 24580
  193.6 5.8 %collective-permute-start.20 = (f32[16,4,1,128]{3,2,1,0:T(1,128)S(1)}, f32[16,4,1,128]{3,2,1,0:T(1,128)S(1)}, u32[]{:S(2)}, u32[]{:S(2)}) collective-permute-start(f32[16,4,1,128]{3,2,1,0:T(1,128)S(1)} %get-tuple-element.28), channel_id=1, source_target_pairs={{4,0},{5,1},{6,2},{7,3},{12,8},{13,9},{14,10},{15,11},{20,16},{21,... | collective-permute-start | bytes 98312 | tf_op jit(solution)/shard_map/ppermute | solution.py:24
  199.7 16.0 %collective-permute-start.22 = (f32[16,4,10,1]{3,2,1,0:T(8,128)S(1)}, f32[16,4,10,1]{3,2,1,0:T(8,128)S(1)}, u32[]{:S(2)}, u32[]{:S(2)}) collective-permute-start(f32[16,4,10,1]{3,2,1,0:T(8,128)S(1)} %get-tuple-element.23), channel_id=1, source_target_pairs={{1,0},{2,1},{3,2},{5,4},{6,5},{7,6},{9,8},{10,9},{11,10},{13,12},{... | collective-permute-start | bytes 7688 | tf_op jit(solution)/shard_map/ppermute | solution.py:24
  201.0 16.4 %collective-permute-start.23 = (f32[16,4,10,1]{3,2,1,0:T(8,128)S(1)}, f32[16,4,10,1]{3,2,1,0:T(8,128)S(1)}, u32[]{:S(2)}, u32[]{:S(2)}) collective-permute-start(f32[16,4,10,1]{3,2,1,0:T(8,128)S(1)} %get-tuple-element.24), channel_id=1, source_target_pairs={{0,1},{1,2},{2,3},{4,5},{5,6},{6,7},{8,9},{9,10},{10,11},{12,13},{... | collective-permute-start | bytes 7688 | tf_op jit(solution)/shard_map/ppermute | solution.py:23
where the time goes:
time: 262 us; the launch traced here: 260 us
  blocking collectives  119 us (45%)
  starting transfers between devices  61.4 us (23%)
  waiting for transfers between devices  58.4 us (22%)
  other arithmetic  14.8 us (6%)
  local copies, waits for them, and re-layouts  3.37 us (1%)
    psum x2, blocking collectives, squares_total(): lax.psum(jnp.sum(residual * residual, axis=(1, 2, 3)), ('gx', 'gy', 'gz'))  78.4 us
    ppermute x12, waiting for transfers between devices, padded_2(): after = lax.ppermute(initial, axis, down)  52.7 us
    psum x1, blocking collectives, shards(): lax.psum(jnp.sum(direction * image, axis=(1, 2, 3)), ('gx', 'gy', 'gz'))  41 us
    ppermute x12, starting transfers between devices, padded_2(): before = lax.ppermute(last, axis, up)  35 us
    ppermute x12, starting transfers between devices, padded_2(): after = lax.ppermute(initial, axis, down)  15.5 us
    all_to_all x1, starting transfers between devices, shards(): lax.all_to_all(outgoing, ('gx', 'gy'), split_axis=1, concat_axis=1, tiled...  5.67 us
    ppermute x12, waiting for transfers between devices, padded_2(): before = lax.ppermute(last, axis, up)  5.64 us
  transfers between devices with their start and end apart: 26, of which 17 were waited for; matrix products, arithmetic and copies ran while one was open for 3% of the time, Pallas kernels for 0%

commit v1 on v0

--- a/solution.py
+++ b/solution.py
@@ -1,11 +1,16 @@
+import functools
+
 import jax
 import jax.numpy as jnp
 from jax import lax
+from jax.experimental import pallas as pl
+from jax.experimental.pallas import tpu as pltpu
 from jax.sharding import PartitionSpec as P
 
 RSTEPS = 2
 CG_ITERS = 2
-
+AXES = ("gx", "gy", "gz")
+LAYER = ("gx", "gy")
 
 time_step = 0.15
 pump_rate = 1.0
@@ -68,10 +73,10 @@
 
 
 def squares_total(residual):
-    return lax.psum(jnp.sum(residual * residual, axis=(1, 2, 3)), ("gx", "gy", "gz"))
-
-
-def shards(
+    return lax.psum(jnp.sum(residual * residual, axis=(1, 2, 3)), AXES)
+
+
+def block_plan(
     concentration,
     pressure_head,
     zone_ids,
@@ -120,10 +125,10 @@
         slot_rank[None, None, :] == slot_ids[None, :, None]
     )
     wanted = jnp.sum(jnp.where(matched, source_tile[None, None, :], 0), axis=2)
-    asked_ids = lax.all_to_all(wanted, ("gx", "gy"), split_axis=0, concat_axis=0, tiled=True)
+    asked_ids = lax.all_to_all(wanted, LAYER, split_axis=0, concat_axis=0, tiled=True)
     outgoing = jnp.take(tile_field, asked_ids.reshape(peer_count * slot_count), axis=1)
     outgoing = outgoing.reshape(solutes, peer_count, slot_count, tile_len)
-    arrived = lax.all_to_all(outgoing, ("gx", "gy"), split_axis=1, concat_axis=1, tiled=True)
+    arrived = lax.all_to_all(outgoing, LAYER, split_axis=1, concat_axis=1, tiled=True)
     arrived_flat = arrived.reshape(solutes, peer_count * slot_count, tile_len)
     fetched = jnp.take(arrived_flat, source_dev * slot_count + slot_rank, axis=1)
     interpolated = jnp.einsum(
@@ -149,7 +154,7 @@
     norm_now = squares_total(residual)
     for iteration in range(CG_ITERS):
         image = apply_operator(direction, flux_terms, mol_coeff, long_coeff)
-        curvature = lax.psum(jnp.sum(direction * image, axis=(1, 2, 3)), ("gx", "gy", "gz"))
+        curvature = lax.psum(jnp.sum(direction * image, axis=(1, 2, 3)), AXES)
         step_size = norm_now / curvature
         solution = solution + spread(step_size) * direction
         residual = residual - spread(step_size) * image
@@ -157,6 +162,270 @@
         direction = residual + spread(norm_next / norm_now) * direction
         norm_now = norm_next
     return (head_now, solution)
+
+
+SMEM = functools.partial(pl.BlockSpec, memory_space=pltpu.SMEM)
+VMEM = functools.partial(pl.BlockSpec, memory_space=pltpu.VMEM)
+
+
+def at_next(v, group, dim, edge):
+    length = v.shape[dim]
+    rolled = pltpu.roll(v, length - 1, dim)
+    ids = lax.broadcasted_iota(jnp.int32, v.shape, dim)
+    count = v.shape[group]
+    beyond = lax.slice_in_dim(rolled, 1, count, axis=group)
+    beyond = jnp.concatenate([beyond, edge], axis=group)
+    return jnp.where(ids == length - 1, beyond, rolled)
+
+
+def at_previous(v, group, dim, edge):
+    rolled = pltpu.roll(v, 1, dim)
+    ids = lax.broadcasted_iota(jnp.int32, v.shape, dim)
+    count = v.shape[group]
+    before = lax.slice_in_dim(rolled, 0, count - 1, axis=group)
+    before = jnp.concatenate([edge, before], axis=group)
+    return jnp.where(ids == 0, before, rolled)
+
+
+def first_of(v, group):
+    return lax.slice_in_dim(v, 0, 1, axis=group)
+
+
+def flow_kernel(shape, me_ref, cond_ref, alpha_ref, cells_ref, flux_ref, head_ref, h_s, q_s, k_s, a_s, w_s):
+    blocks_x, blocks_y, blocks_z, cells_x = shape
+    per = blocks_y * blocks_z
+    planes = blocks_x * cells_x
+    plane_shape = h_s.shape[1:]
+    zones = cond_ref.shape[0]
+    roots = [jnp.sqrt(jnp.full((1, 1, 1, 1), cond_ref[n], jnp.float32)) for n in range(zones)]
+    for plane in range(planes):
+        a, i = plane // cells_x, plane % cells_x
+        head = cells_ref[a * per : (a + 1) * per, 0, i].reshape(plane_shape)
+        code = cells_ref[a * per : (a + 1) * per, 1, i].reshape(plane_shape)
+        well = jnp.where(code >= zones, 1.0, 0.0)
+        zone = code - zones * well
+        root = jnp.broadcast_to(roots[0], plane_shape)
+        half = jnp.full(plane_shape, 0.5 * alpha_ref[0], jnp.float32)
+        for n in range(1, zones):
+            root = jnp.where(zone == n, roots[n], root)
+            half = jnp.where(zone == n, 0.5 * alpha_ref[n], half)
+        h_s[plane] = head
+        k_s[plane] = root
+        a_s[plane] = half
+        w_s[plane] = well
+        q_s[plane] = root * jnp.exp(half * head)
+    none_y = jnp.zeros((1,) + plane_shape[1:], jnp.float32)
+    none_z = jnp.zeros(plane_shape[:1] + (1,) + plane_shape[2:], jnp.float32)
+    for sweep in range(RSTEPS):
+        if sweep > 0:
+            for plane in range(planes):
+                q_s[plane] = k_s[plane] * jnp.exp(a_s[plane] * h_s[plane])
+        from_below = jnp.zeros(plane_shape, jnp.float32)
+        for plane in range(planes):
+            h, q = h_s[plane], q_s[plane]
+            if plane < planes - 1:
+                in_x = q * q_s[plane + 1] * (h_s[plane + 1] - h)
+            else:
+                in_x = jnp.zeros(plane_shape, jnp.float32)
+            in_y = q * at_next(q, 0, 2, none_y) * (at_next(h, 0, 2, none_y) - h)
+            in_z = q * at_next(q, 1, 3, none_z) * (at_next(h, 1, 3, none_z) - h + gravity_sign[4])
+            net = in_x - from_below + (in_y - at_previous(in_y, 0, 2, none_y))
+            net = net + (in_z - at_previous(in_z, 1, 3, none_z))
+            h_s[plane] = h + time_step * (net - pump_rate * w_s[plane])
+            from_below = in_x
+            if sweep == RSTEPS - 1:
+                flux_ref[0, plane] = jnp.sqrt(1.0 + in_x * in_x)
+                flux_ref[1, plane] = jnp.sqrt(1.0 + in_y * in_y)
+                flux_ref[2, plane] = jnp.sqrt(1.0 + in_z * in_z)
+    mine_x, mine_y, mine_z = me_ref[0], me_ref[1], me_ref[2]
+    for i in range(cells_x):
+        head_ref[i] = h_s[mine_x * cells_x + i, mine_y, mine_z]
+
+
+def interpolate_kernel(copies, from_ref, to_ref, tiles_ref, weights_ref, conc_ref, out_ref, sum_s):
+    entries = weights_ref.shape[0]
+    solutes, tile_count, tile_len = conc_ref.shape
+    sum_s[...] = jnp.zeros_like(sum_s)
+    for e in range(entries):
+        got = jnp.dot(tiles_ref[from_ref[e]], weights_ref[e], preferred_element_type=jnp.float32)
+        rows = pl.ds(pl.multiple_of(to_ref[e] * solutes, solutes), solutes)
+        sum_s[rows, :] = sum_s[rows, :] + got
+    for s in range(solutes):
+        added = sum_s[pl.ds(s, tile_count, stride=solutes), :]
+        field = conc_ref[s].astype(jnp.float32) + added
+        for n in range(copies):
+            out_ref[s * copies + n] = field
+
+
+def spread_out(v, above, below_x, fluxes, mol, lng, edge_w):
+    w_x, w_y, w_z = [mol + lng * f for f in fluxes]
+    if above is None:
+        f_x = w_x * v
+    else:
+        f_x = w_x * (v - above)
+    if below_x is None:
+        below_x = -edge_w * v
+    none_y = jnp.zeros((1,) + v.shape[1:], jnp.float32)
+    none_z = jnp.zeros(v.shape[:1] + (1,) + v.shape[2:], jnp.float32)
+    f_y = w_y * (v - at_next(v, 0, 2, none_y))
+    f_z = w_z * (v - at_next(v, 1, 3, none_z))
+    low_y = -edge_w * first_of(v, 0)
+    low_z = -edge_w * first_of(v, 1)
+    out = f_x - below_x + (f_y - at_previous(f_y, 0, 2, low_y))
+    return out + (f_z - at_previous(f_z, 1, 3, low_z)), f_x
+
+
+def solve_kernel(shape, me_ref, mol_ref, long_ref, field_ref, flux_ref, out_ref, y_s):
+    blocks_x, blocks_y, blocks_z, cells_x = shape
+    per = blocks_y * blocks_z
+    planes = blocks_x * cells_x
+    plane_shape = flux_ref.shape[2:]
+    solute, part = me_ref[3], me_ref[4]
+    mol = disp_time * mol_ref[solute]
+    lng = disp_time * long_ref[solute]
+    edge_w = mol + lng
+
+    def plane_of(ref, plane):
+        a, i = plane // cells_x, plane % cells_x
+        return ref[a * per : (a + 1) * per, i].reshape(plane_shape)
+
+    def total(x):
+        return jnp.sum(x, axis=(0, 1))
+
+    p = [jnp.zeros(plane_shape[2:], jnp.float32) for _ in range(4)]
+    below = None
+    for plane in range(planes):
+        a, i = plane // cells_x, plane % cells_x
+        v = plane_of(field_ref, plane)
+        above = plane_of(field_ref, plane + 1) if plane < planes - 1 else None
+        fluxes = [flux_ref[n, plane] for n in range(3)]
+        y, below = spread_out(v, above, below, fluxes, mol, lng, edge_w)
+        y_s[a * per : (a + 1) * per, i] = y.reshape((per,) + plane_shape[2:])
+        p[0] += total(v * v)
+        p[1] += total(v * y)
+        p[2] += total(y * y)
+    below = None
+    for plane in range(planes):
+        v = plane_of(y_s, plane)
+        above = plane_of(y_s, plane + 1) if plane < planes - 1 else None
+        fluxes = [flux_ref[n, plane] for n in range(3)]
+        z, below = spread_out(v, above, below, fluxes, mol, lng, edge_w)
+        p[3] += total(v * z)
+    p0, p1, p2, p3 = [jnp.sum(x, axis=(0, 1), keepdims=True) for x in p]
+    d = p1 / p0
+    a0 = 1.0 / (1.0 + d)
+    var = p2 - d * p1
+    wid = p3 - 2.0 * d * p2 + d * d * p1
+    ratio = var / p0
+    a1 = var / (var + wid - a0 * var * ratio)
+    c0 = a0 + a1 * (a0 * d + a0 * a0 * ratio)
+    c1 = a1 * a0
+    rows = out_ref.shape[1]
+    for n in range(rows):
+        i = part * rows + n
+        out_ref[:, n] = c0[None] * field_ref[:, i] - c1[None] * y_s[:, i]
+
+
+def field_plan(
+    concentration,
+    pressure_head,
+    zone_ids,
+    well_cells,
+    zone_conductivity,
+    zone_alpha,
+    disp_molecular,
+    disp_longitudinal,
+    entry_counts,
+    dest_tiles,
+    source_devices,
+    source_tiles,
+    interp_weights,
+):
+    blocks_x, blocks_y, blocks_z = (lax.axis_size(axis) for axis in AXES)
+    devices = blocks_x * blocks_y * blocks_z
+    peers = blocks_x * blocks_y
+    solutes, cells_x, cells_y, tile_len = concentration.shape
+    tile_count = cells_x * cells_y
+    entries = dest_tiles.shape[-1]
+    zones = zone_conductivity.shape[0]
+    copies = devices // solutes
+    shape = (blocks_x, blocks_y, blocks_z, cells_x)
+    plane_shape = (blocks_y, blocks_z, cells_y, tile_len)
+    planes = blocks_x * cells_x
+    f32 = jnp.float32
+
+    ix, iy, iz = (lax.axis_index(axis) for axis in AXES)
+    number = (ix * blocks_y + iy) * blocks_z + iz
+    me = jnp.stack([ix, iy, iz, number // copies, number % copies]).astype(jnp.int32)
+
+    tiles = concentration.reshape(solutes, tile_count, tile_len)
+    by_tile = tiles.transpose(1, 0, 2)
+    by_tile = jnp.broadcast_to(by_tile[None], (peers,) + by_tile.shape)
+    layer = lax.all_to_all(by_tile, LAYER, split_axis=0, concat_axis=0, tiled=True)
+
+    code = (zone_ids + zones * well_cells).astype(f32)
+    cells = jnp.stack([pressure_head, code])
+    cells = jnp.broadcast_to(cells[None], (devices,) + cells.shape)
+    cells = lax.all_to_all(cells, AXES, split_axis=0, concat_axis=0, tiled=True)
+
+    entry_ids = jnp.arange(entries, dtype=jnp.int32)
+    from_tile = source_devices.reshape(entries) * tile_count + source_tiles.reshape(entries)
+    to_tile = jnp.where(
+        entry_ids < entry_counts.reshape(()), dest_tiles.reshape(entries), tile_count
+    )
+    fields = pl.pallas_call(
+        functools.partial(interpolate_kernel, copies),
+        out_shape=jax.ShapeDtypeStruct((devices, tile_count, tile_len), f32),
+        in_specs=[SMEM(), SMEM(), VMEM(), VMEM(), VMEM()],
+        out_specs=VMEM(),
+        scratch_shapes=[pltpu.VMEM(((tile_count + 1) * solutes, tile_len), f32)],
+        name="interpolate",
+    )(
+        from_tile,
+        to_tile,
+        layer.reshape(peers * tile_count, solutes, tile_len),
+        interp_weights.reshape(entries, tile_len, tile_len),
+        tiles,
+    )
+    field = lax.all_to_all(fields, AXES, split_axis=0, concat_axis=0, tiled=True)
+    field = field.reshape(devices, cells_x, cells_y, tile_len)
+
+    grid_scratch = pltpu.VMEM((planes,) + plane_shape, f32)
+    flux, head = pl.pallas_call(
+        functools.partial(flow_kernel, shape),
+        out_shape=(
+            jax.ShapeDtypeStruct((3, planes) + plane_shape, f32),
+            jax.ShapeDtypeStruct((cells_x, cells_y, tile_len), f32),
+        ),
+        in_specs=[SMEM(), SMEM(), SMEM(), VMEM()],
+        out_specs=(VMEM(), VMEM()),
+        scratch_shapes=[grid_scratch] * 5,
+        name="flow",
+    )(me, zone_conductivity, zone_alpha, cells)
+
+    rows = cells_x // copies
+    back = pl.pallas_call(
+        functools.partial(solve_kernel, shape),
+        out_shape=jax.ShapeDtypeStruct((devices, rows, cells_y, tile_len), f32),
+        in_specs=[SMEM(), SMEM(), SMEM(), VMEM(), VMEM()],
+        out_specs=VMEM(),
+        scratch_shapes=[pltpu.VMEM((devices, cells_x, cells_y, tile_len), f32)],
+        name="solve",
+    )(me, disp_molecular, disp_longitudinal, field, flux)
+    back = lax.all_to_all(back, AXES, split_axis=0, concat_axis=0, tiled=True)
+    return head, back.reshape(solutes, cells_x, cells_y, tile_len)
+
+
+def shards(concentration, *rest):
+    solutes, cells_x, cells_y, tile_len = concentration.shape
+    devices = 1
+    for axis in AXES:
+        devices *= lax.axis_size(axis)
+    copies = devices // solutes
+    even = devices % solutes == 0 and copies > 0 and cells_x % copies == 0
+    if even and cells_y == 8 and tile_len == 128:
+        return field_plan(concentration, *rest)
+    return block_plan(concentration, *rest)
 
 
 def solution(mesh):

time: 262 us -> 66.2 us (0.25)
  blocking collectives: 119 us -> 10.4 us
  starting transfers between devices: 61.4 us -> 12.4 us
  waiting for transfers between devices: 58.4 us -> 26 us
  other arithmetic: 14.8 us -> 1.93 us
  Pallas kernels: 0 us -> 8.87 us
    psum x3 -> x0, blocking collectives: 119 us -> none  [the longest x2 78.4 us: squares_total(): lax.psum(jnp.sum(residual * residual, axis=(1, 2, 3)), ('gx', 'gy', 'gz'))]
    ppermute x24 -> x0, waiting for transfers between devices: 58.4 us -> none  [the longest x12 52.7 us: padded_2(): after = lax.ppermute(initial, axis, down)]
    ppermute x24 -> x0, starting transfers between devices: 50.5 us -> none  [the longest x12 35 us: padded_2(): before = lax.ppermute(last, axis, up)]
    all_to_all x2 -> x3, waiting for transfers between devices: 0.01 us -> 26 us  [the longest x1 11.4 us: field_plan(): cells = lax.all_to_all(cells, AXES, split_axis=0, concat_axis=0, tiled=True)]
    all_to_all x0 -> x1, blocking collectives: none -> 10.4 us  [field_plan(): back = lax.all_to_all(back, AXES, split_axis=0, concat_axis=0, tiled=True)]
    pallas_call x0 -> x3, Pallas kernels: none -> 8.87 us  [the longest x1 3.17 us: field_plan(): pl.pallas_call(functools.partial(flow_kernel, shape), out_shape=(jax.Shap...]
    reduce_sum x6 -> x0, other arithmetic: 4.58 us -> none  [the longest x1 1.46 us: shards(): wanted = jnp.sum(jnp.where(matched, source_tile[None, None, :], 0), axis=2)]
    all_to_all x2 -> x3, starting transfers between devices: 10.9 us -> 12.4 us  [the longest x1 5.2 us: field_plan(): lax.all_to_all(by_tile, LAYER, split_axis=0, concat_axis=0, tiled=True)]
  transfers between devices with their start and end apart: 26 -> 3, of which waited for: 17 -> 3; matrix products, arithmetic and copies ran while one was open for 3% -> 4% of each run, Pallas kernels for 0% -> 10%
where the time goes in v1:
time: 66.2 us; the launch traced here: 65.6 us
  waiting for transfers between devices  26 us (39%)
  starting transfers between devices  12.4 us (19%)
  blocking collectives  10.4 us (16%)
  Pallas kernels  8.87 us (13%)
  local copies, waits for them, and re-layouts  4.74 us (7%)
  other arithmetic  1.93 us (3%)
  between operations  1.38 us (2%)
    all_to_all x1, waiting for transfers between devices, field_plan(): cells = lax.all_to_all(cells, AXES, split_axis=0, concat_axis=0, tiled=True)  11.4 us
    all_to_all x1, blocking collectives, field_plan(): back = lax.all_to_all(back, AXES, split_axis=0, concat_axis=0, tiled=True)  10.4 us
    all_to_all x1, waiting for transfers between devices, field_plan(): lax.all_to_all(by_tile, LAYER, split_axis=0, concat_axis=0, tiled=True)  7.72 us
    all_to_all x1, waiting for transfers between devices, field_plan(): lax.all_to_all(fields, AXES, split_axis=0, concat_axis=0, tiled=True)  6.87 us
    all_to_all x1, starting transfers between devices, field_plan(): lax.all_to_all(by_tile, LAYER, split_axis=0, concat_axis=0, tiled=True)  5.2 us
    all_to_all x1, starting transfers between devices, field_plan(): cells = lax.all_to_all(cells, AXES, split_axis=0, concat_axis=0, tiled=True)  4.59 us
    pallas_call x1, Pallas kernels, field_plan(): pl.pallas_call(functools.partial(flow_kernel, shape), out_shape=(jax.Shap...  3.17 us
    pallas_call x1, Pallas kernels, field_plan(): pl.pallas_call(functools.partial(interpolate_kernel, copies), out_shape=j...  3.11 us
  transfers between devices with their start and end apart: 3, of which 3 were waited for; matrix products, arithmetic and copies ran while one was open for 4% of the time, Pallas kernels for 10%

profile of v1, /device:TPU:0, one launch (start us, length us, event | category | flops | bytes accessed | tf_op | source)
XLA Modules:
  0.0 65.6 jit_solution(15406362913870350570)
XLA Ops:
  0.6 0.0 copy-start.4
  0.6 0.0 copy-start.5
  0.7 0.0 copy-start.3
  0.7 0.9 %copy.15 = bf16[16,16,128]{2,1,0:T(8,128)(2,1)S(1)} copy(bf16[16,16,128]{2,0,1:T(8,128)(2,1)} %bitcast.27) | data formatting | bytes 131072 | tf_op jit(solution)/shard_map/transpose | solution.py:362
  1.5 0.9 %broadcast_in_dim.6 = bf16[8,16,16,128]{3,2,1,0:T(8,128)(2,1)} broadcast(bf16[16,16,128]{2,1,0:T(8,128)(2,1)S(1)} %copy.15), dimensions={1,2,3} | broadcast | bytes 589824 | tf_op jit(solution)/shard_map/broadcast_in_dim | solution.py:363
  2.4 5.2 %all-to-all-start.1 = ((bf16[8,16,16,128]{3,2,1,0:T(8,128)(2,1)}), bf16[8,16,16,128]{3,2,1,0:T(8,128)(2,1)S(1)}, u32[]{:S(2)}, u32[]{:S(2)}) async-start(bf16[8,16,16,128]{3,2,1,0:T(8,128)(2,1)} %broadcast_in_dim.6), calls=%async_computation.1 | async-start | bytes 1048576 | tf_op jit(solution)/shard_map/all_to_all | solution.py:364
  7.6 0.7 %convert_bitcast_fusion = f32[1,2,8,128]{3,2,1,0:T(8,128)S(1)} fusion(s32[2,8,128]{2,1,0:T(8,128)} %param.15, s32[2,8,128]{2,1,0:T(8,128)} %param.16), kind=kLoop, calls=%fused_computation.1 | loop fusion | flops 6144 | bytes 24576 | tf_op jit(solution)/shard_map/stack | solution.py:367
  8.3 0.7 %pad_maximum_fusion = f32[2,2,8,128]{3,2,1,0:T(8,128)S(1)} fusion(f32[1,2,8,128]{3,2,1,0:T(8,128)S(1)} %convert_bitcast_fusion, f32[1,2,8,128]{3,2,1,0:T(8,128)} %bitcast.29), kind=kLoop, calls=%fused_computation | loop fusion | flops 4096 | bytes 32768 | tf_op jit(solution)/shard_map/stack | solution.py:367
  9.0 7.7 %all-to-all-done.1 = bf16[8,16,16,128]{3,2,1,0:T(8,128)(2,1)S(1)} async-done(((bf16[8,16,16,128]{3,2,1,0:T(8,128)(2,1)}), bf16[8,16,16,128]{3,2,1,0:T(8,128)(2,1)S(1)}, u32[]{:S(2)}, u32[]{:S(2)}) %all-to-all-start.1) | async-done | bytes 524320 | tf_op jit(solution)/shard_map/all_to_all | solution.py:364
  16.7 0.0 copy-start.1
  16.7 0.9 %broadcast_in_dim.5 = f32[32,2,2,8,128]{4,3,2,1,0:T(8,128)} broadcast(f32[2,2,8,128]{3,2,1,0:T(8,128)S(1)} %pad_maximum_fusion), dimensions={1,2,3,4} | broadcast | bytes 540672 | tf_op jit(solution)/shard_map/broadcast_in_dim | solution.py:368
  17.7 4.6 %all-to-all-start = ((f32[32,2,2,8,128]{4,3,2,1,0:T(8,128)}), f32[32,2,2,8,128]{4,3,2,1,0:T(8,128)S(1)}, u32[]{:S(2)}, u32[]{:S(2)}) async-start(f32[32,2,2,8,128]{4,3,2,1,0:T(8,128)} %broadcast_in_dim.5), calls=%async_computation | async-start | bytes 1048576 | tf_op jit(solution)/shard_map/all_to_all | solution.py:369
  22.9 0.0 copy-done.4
  22.9 0.0 copy-done.5
  22.9 0.0 copy-done.3
  22.9 0.5 compare_select_fusion
  23.5 0.0 copy-done.1
  23.5 3.1 %interpolate.1 = f32[32,16,128]{2,1,0:T(8,128)} custom-call(s32[64]{0:T(128)} %get-tuple-element.7.from_ref, s32[64]{0:T(128)} %get-tuple-element.6.to_ref, bf16[128,16,128]{2,1,0:T(8,128)(2,1)} %bitcast.24, bf16[64,128,128]{2,1,0:T(8,128)(2,1)} %bitcast.23, bf16[16,16,128]{2,1,0:T(8,128)(2,1)} %bitcast.28), custom_call_target="tpu_custom_call" | custom-call | tf_op jit(solution)/shard_map/interpolate/pallas_call | solution.py:376
  26.6 11.4 %all-to-all-done.cells_ref = f32[32,2,2,8,128]{4,3,2,1,0:T(8,128)S(1)} async-done(((f32[32,2,2,8,128]{4,3,2,1,0:T(8,128)}), f32[32,2,2,8,128]{4,3,2,1,0:T(8,128)S(1)}, u32[]{:S(2)}, u32[]{:S(2)}) %all-to-all-start) | async-done | bytes 524320 | tf_op jit(solution)/shard_map/all_to_all | solution.py:369
  38.0 0.0 copy-start
  38.0 2.6 %all-to-all-start.2 = ((f32[32,16,128]{2,1,0:T(8,128)}), f32[32,16,128]{2,1,0:T(8,128)S(1)}, u32[]{:S(2)}, u32[]{:S(2)}) async-start(f32[32,16,128]{2,1,0:T(8,128)} %interpolate.1), calls=%async_computation.2 | async-start | bytes 524288 | tf_op jit(solution)/shard_map/all_to_all | solution.py:390
  40.6 0.7 %stack.32.me_ref = s32[5]{0:T(128)} concatenate(s32[1]{0:T(128)} %bitcast, s32[1]{0:T(128)} %bitcast.1, s32[1]{0:T(128)} %bitcast.2, s32[1]{0:T(128)} %bitcast.3, s32[1]{0:T(128)} %bitcast.4), dimensions={0} | concatenate | bytes 40 | tf_op jit(solution)/shard_map/stack | solution.py:359
  41.3 0.0 copy-done
  41.3 3.2 %flow.1 = (f32[3,8,2,4,8,128]{5,4,3,2,1,0:T(8,128)}, f32[2,8,128]{2,1,0:T(8,128)}) custom-call(s32[5]{0:T(128)} %stack.32.me_ref, f32[8]{0:T(128)} %cond_ref.1, f32[8]{0:T(128)} %alpha_ref.1, f32[32,2,2,8,128]{4,3,2,1,0:T(8,128)} %copy-done), custom_call_target="tpu_custom_call" | custom-call | tf_op jit(solution)/shard_map/flow/pallas_call | solution.py:394
  44.4 6.9 %all-to-all-done.2 = f32[32,16,128]{2,1,0:T(8,128)S(1)} async-done(((f32[32,16,128]{2,1,0:T(8,128)}), f32[32,16,128]{2,1,0:T(8,128)S(1)}, u32[]{:S(2)}, u32[]{:S(2)}) %all-to-all-start.2) | async-done | bytes 262176 | tf_op jit(solution)/shard_map/all_to_all | solution.py:390
  51.3 0.0 copy-start.2
  51.3 0.7 %copy-done.2 = f32[32,16,128]{2,1,0:T(8,128)} copy-done((f32[32,16,128]{2,1,0:T(8,128)}, f32[32,16,128]{2,1,0:T(8,128)S(1)}, u32[]{:S(2)}) %copy-start.2) | copy-done | bytes 262168
  52.0 2.6 %solve.1 = f32[32,1,8,128]{3,2,1,0:T(8,128)} custom-call(s32[5]{0:T(128)} %stack.32.me_ref, f32[16]{0:T(128)} %mol_ref.1, f32[16]{0:T(128)} %long_ref.1, f32[32,2,8,128]{3,2,1,0:T(8,128)} %bitcast.25, f32[3,8,2,4,8,128]{5,4,3,2,1,0:T(8,128)} %get-tuple-element.5.flux_ref), custom_call_target="tpu_custom_call" | custom-call | tf_op jit(solution)/shard_map/solve/pallas_call | solution.py:407
  54.6 10.4 %all_to_all.20 = f32[32,1,8,128]{3,2,1,0:T(8,128)S(1)} all-to-all(f32[32,1,8,128]{3,2,1,0:T(8,128)} %solve.1), channel_id=1, replica_groups=mesh['gx'=4,'gy'=2,'gz'=4] {'gx','gy','gz'}, dimensions={0} | all-to-all | bytes 262144 | tf_op jit(solution)/shard_map/all_to_all | solution.py:415
  65.0 0.7 copy.18
Async XLA Ops:
  0.6 22.3 %copy-start.4 = (s32[1,1,1,64]{3,2,1,0:T(1,128)S(1)}, s32[1,1,1,64]{3,2,1,0:T(1,128)}, u32[]{:S(2)}) copy-start(s32[1,1,1,64]{3,2,1,0:T(1,128)} %param.24) | copy-start | bytes 772
  0.6 22.3 %copy-start.5 = (s32[1,1,1,64,1]{3,4,2,1,0:T(1,128)S(1)}, s32[1,1,1,64,1]{3,4,2,1,0:T(1,128)}, u32[]{:S(2)}) copy-start(s32[1,1,1,64,1]{3,4,2,1,0:T(1,128)} %param.23) | copy-start | bytes 772
  0.7 22.3 %copy-start.3 = (s32[1,1,1,64]{3,2,1,0:T(1,128)S(1)}, s32[1,1,1,64]{3,2,1,0:T(1,128)}, u32[]{:S(2)}) copy-start(s32[1,1,1,64]{3,2,1,0:T(1,128)} %param.22) | copy-start | bytes 772
  2.4 14.3 %all-to-all-start.1 = ((bf16[8,16,16,128]{3,2,1,0:T(8,128)(2,1)}), bf16[8,16,16,128]{3,2,1,0:T(8,128)(2,1)S(1)}, u32[]{:S(2)}, u32[]{:S(2)}) async-start(bf16[8,16,16,128]{3,2,1,0:T(8,128)(2,1)} %broadcast_in_dim.6), calls=%async_computation.1 | async-start | bytes 1048576 | tf_op jit(solution)/shard_map/all_to_all | solution.py:364
  16.7 6.7 %copy-start.1 = (bf16[8,16,16,128]{3,2,1,0:T(8,128)(2,1)}, bf16[8,16,16,128]{3,2,1,0:T(8,128)(2,1)S(1)}, u32[]{:S(2)}) copy-start(bf16[8,16,16,128]{3,2,1,0:T(8,128)(2,1)S(1)} %all-to-all-done.1) | copy-start | bytes 1572868
  17.7 20.3 %all-to-all-start = ((f32[32,2,2,8,128]{4,3,2,1,0:T(8,128)}), f32[32,2,2,8,128]{4,3,2,1,0:T(8,128)S(1)}, u32[]{:S(2)}, u32[]{:S(2)}) async-start(f32[32,2,2,8,128]{4,3,2,1,0:T(8,128)} %broadcast_in_dim.5), calls=%async_computation | async-start | bytes 1048576 | tf_op jit(solution)/shard_map/all_to_all | solution.py:369
  38.0 3.3 %copy-start = (f32[32,2,2,8,128]{4,3,2,1,0:T(8,128)}, f32[32,2,2,8,128]{4,3,2,1,0:T(8,128)S(1)}, u32[]{:S(2)}) copy-start(f32[32,2,2,8,128]{4,3,2,1,0:T(8,128)S(1)} %all-to-all-done.cells_ref) | copy-start | bytes 1572868
  38.0 13.3 %all-to-all-start.2 = ((f32[32,16,128]{2,1,0:T(8,128)}), f32[32,16,128]{2,1,0:T(8,128)S(1)}, u32[]{:S(2)}, u32[]{:S(2)}) async-start(f32[32,16,128]{2,1,0:T(8,128)} %interpolate.1), calls=%async_computation.2 | async-start | bytes 524288 | tf_op jit(solution)/shard_map/all_to_all | solution.py:390
  51.3 0.7 %copy-start.2 = (f32[32,16,128]{2,1,0:T(8,128)}, f32[32,16,128]{2,1,0:T(8,128)S(1)}, u32[]{:S(2)}) copy-start(f32[32,16,128]{2,1,0:T(8,128)S(1)} %all-to-all-done.2) | copy-start | bytes 786436
